TPU v7x, 128 devices: a whole 4x4x4 slice. The times are simulated.
128 devices in a mesh: chan: 16 (over z, y_hi, core), win: 8 (over x, y_lo).
Axes of the slice: x: 4, y: 4 (y_hi: 2, y_lo: 2; y = y_hi * 2 + y_lo), z: 4, core: 2. Of those that a mesh axis runs over, the one named last changes fastest.
Arguments:
- waves: float32 [1024, 16384], P('chan', 'win'), may hold values from -40 to 40
- matchings: int32 [3, 16], replicated, may hold values from 0 to 15, as said below
- lag_offset: int32 [3, 16], replicated, may hold values from -64 to 64
Outputs:
- stacked: float32 [64, 3, 1024, 256], P('win', None, 'chan')
Inputs may be any that keep to these rules, and one draw needn't show every extreme that they name: `matchings`: each row pairs the 16 blocks two by two: the partner of a block's partner is the block itself, and no block is its own partner.
All inputs are finite; a program needn't handle non-finite values.
Results may differ from a plain program's by a relative error of at most 0.012.
Values may be sent and summed in bfloat16 or wider, within the bound.
No kernel may reach another device: no remote copies, remote signals or barrier semaphores. Data moves between devices by JAX's collectives and lax.ppermute only.
A program may use at most 128 MiB of HBM per device.

v0:
```python
import jax
import jax.numpy as jnp
from jax import lax
from jax.experimental import pallas as pl
from jax.experimental.pallas import tpu as pltpu
from jax.sharding import PartitionSpec as P

CHANS = 64
LEN = 2048
HALF = LEN // 2
BLOCKS = 16
WINS = 8
MATCH = 3
LAGS = 256
ROWS = CHANS // WINS
FINE = 16
GROUPS = 128 // FINE
SPAN = LEN + 128
WIDE = LEN + 512
PAD = 96
PAIR = 2
SCALE = 1.0 / 128.0


def whiten_kernel(x_ref, cut_ref, turned_ref):
    x = x_ref[...]
    power = jnp.mean(x * x, axis=1, keepdims=True)
    white = x / jnp.sqrt(power + 1e-06)
    for c in range(BLOCKS):
        for g in range(WINS):
            cut_ref[c, g] = white[g * ROWS:(g + 1) * ROWS, 128 * c:128 * (c + 1)].astype(jnp.bfloat16)
    halves = jnp.concatenate([white[:, :HALF], white[:, HALF:]], axis=0)
    turned_ref[...] = halves.T.astype(jnp.bfloat16)


def whiten(x):
    return pl.pallas_call(
        whiten_kernel,
        out_shape=(
            jax.ShapeDtypeStruct((BLOCKS, WINS, ROWS, 128), jnp.bfloat16),
            jax.ShapeDtypeStruct((HALF, 128), jnp.bfloat16),
        ),
        compiler_params=pltpu.CompilerParams(vmem_limit_bytes=4 << 20),
        name="whiten",
    )(x)


def choose_kernel(match_ref, from_ref, to_ref):
    for d in range(BLOCKS):
        for m in range(MATCH):
            to_ref[d, m] = from_ref[match_ref[m, d]]


def choose(matchings, chunks):
    return pl.pallas_call(
        choose_kernel,
        out_shape=jax.ShapeDtypeStruct((BLOCKS, MATCH, WINS, ROWS, 128), jnp.bfloat16),
        in_specs=[pl.BlockSpec(memory_space=pltpu.SMEM), pl.BlockSpec(memory_space=pltpu.VMEM)],
        compiler_params=pltpu.CompilerParams(vmem_limit_bytes=4 << 20),
        name="choose",
    )(matchings, chunks)


def corr_kernel(offs, s0_ref, s1_ref, s2_ref, s3_ref, t_ref, o_ref, y0, y1, ts0, ts1, acc):
    lane = lax.broadcasted_iota(jnp.int32, (1, 128), 1)
    mine = offs[MATCH]
    sources = (s0_ref, s1_ref, s2_ref, s3_ref)

    def source(r, y):
        for n in range(PAIR):
            x = sources[r][n].astype(jnp.float32)
            swapped = pltpu.roll(x, CHANS, 1)
            gap = jnp.zeros((FINE, 128), jnp.float32)
            now = jnp.concatenate([x, swapped, gap], axis=0)
            late = jnp.concatenate([gap, swapped, x], axis=0)
            y[n, PAD:PAD + LEN + FINE, :] = jnp.where(lane < CHANS, now, late).astype(jnp.bfloat16)

    def partner(r, ts):
        zeros = jnp.zeros((ROWS, 256), jnp.float32)
        for n in range(PAIR):
            w = lax.bitwise_xor(mine, 2 * r + n)
            for m in range(MATCH):
                cut = [t_ref[c, m, w].astype(jnp.float32) for c in range(BLOCKS)]
                row = jnp.concatenate([zeros] + cut + [zeros], axis=1)
                even = pltpu.roll(row, WIDE - 128 - offs[m], 1)
                odd = pltpu.roll(even, WIDE - 1, 1)
                both = jnp.concatenate([even, odd], axis=0).astype(jnp.bfloat16)
                for k in range(FINE // 2):
                    first = 128 * m + 16 * k
                    ts[n, first:first + 16, :] = both[:, 2 * k:2 * k + SPAN + 128]

    def product(y, ts, fresh):
        lhs = jnp.concatenate(
            [
                jnp.concatenate([ts[n, :, 128 * top:128 * top + SPAN] for n in range(PAIR)], axis=1)
                for top in range(2)
            ],
            axis=0,
        )
        rhs = jnp.concatenate(
            [
                jnp.concatenate([y[n, PAD - 2 * FINE * q:PAD - 2 * FINE * q + SPAN, :] for n in range(PAIR)], axis=0)
                for q in range(GROUPS // 2)
            ],
            axis=1,
        )
        r = jnp.dot(lhs, rhs, preferred_element_type=jnp.float32)
        for q in range(GROUPS // 2):
            part = r[:, 128 * q:128 * (q + 1)]
            acc[q] = part if fresh else acc[q] + part

    for y in (y0, y1):
        for n in range(PAIR):
            y[n, :PAD, :] = jnp.zeros((PAD, 128), jnp.bfloat16)
            y[n, PAD + LEN + FINE:, :] = jnp.zeros((SPAN - LEN - FINE, 128), jnp.bfloat16)
    buffers = ((y0, ts0), (y1, ts1))
    rounds = WINS // PAIR
    source(0, y0)
    partner(0, ts0)
    for r in range(rounds):
        if r + 1 < rounds:
            source(r + 1, buffers[(r + 1) % 2][0])
            partner(r + 1, buffers[(r + 1) % 2][1])
        product(*buffers[r % 2], r == 0)

    for top in range(2):
        for m in range(MATCH):
            for b in range(0, ROWS, 2):
                base = (top * MATCH + m) * 128 + b
                rows = []
                for q in range(GROUPS // 2):
                    lo = acc[q, pl.ds(base, FINE, stride=ROWS), :] * SCALE
                    hi = acc[q, pl.ds(base + 1, FINE, stride=ROWS), :] * SCALE
                    rows.append(jnp.where(lane < CHANS, lo, pltpu.roll(hi, CHANS, 1)))
                    rows.append(jnp.where(lane < CHANS, pltpu.roll(lo, CHANS, 1), hi))
                z = jnp.concatenate(rows, axis=0).T
                o_ref[b, m, :, 128 * top:128 * (top + 1)] = z[:CHANS]
                o_ref[b + 1, m, :, 128 * top:128 * (top + 1)] = z[CHANS:]


def corr(offs, sources, partner):
    vmem = pl.BlockSpec(memory_space=pltpu.VMEM)
    return pl.pallas_call(
        corr_kernel,
        out_shape=jax.ShapeDtypeStruct((ROWS, MATCH, CHANS, LAGS), jnp.float32),
        in_specs=[pl.BlockSpec(memory_space=pltpu.SMEM)] + [vmem] * 5,
        out_specs=vmem,
        scratch_shapes=[pltpu.VMEM((PAIR, PAD + SPAN, 128), jnp.bfloat16)] * 2
        + [pltpu.VMEM((PAIR, MATCH * FINE * ROWS, SPAN + 128), jnp.bfloat16)] * 2
        + [pltpu.VMEM((GROUPS // 2, 2 * MATCH * FINE * ROWS, 128), jnp.float32)],
        compiler_params=pltpu.CompilerParams(vmem_limit_bytes=28 << 20),
        name="corr",
    )(offs, *sources, partner)


def local(waves, matchings, lag_offset):
    win = lax.axis_index("win")
    offs = lax.dynamic_index_in_dim(lag_offset, lax.axis_index("chan"), 1, keepdims=False)
    offs = jnp.concatenate([offs, jnp.full((1,), win, jnp.int32)])
    cut, turned = whiten(waves)
    chunks = lax.all_to_all(cut.reshape(BLOCKS * WINS, ROWS, 128), ("chan", "win"), 0, 0)
    other = lax.ppermute(turned, "win", [(i, i ^ 1) for i in range(WINS)])
    pair = jnp.stack([turned, other])
    far = []
    for r in (1, 2, 3):
        far.append(lax.ppermute(pair, "win", [(i, i ^ (2 * r)) for i in range(WINS)]))
    sent = choose(matchings, chunks.reshape(BLOCKS, WINS, ROWS, 128))
    partner = lax.all_to_all(sent, "chan", 0, 0)
    return corr(offs, [pair] + far, partner)


def solution(mesh):
    return jax.shard_map(
        local,
        mesh=mesh,
        in_specs=(P("chan", "win"), P(), P()),
        out_specs=P("win", None, "chan", None),
        check_vma=False,
    )
```

profile of v0, /device:TPU:1, one launch (start us, length us, event | category | flops | bytes accessed | tf_op | source)
XLA Modules:
  0.0 74.0 jit_solution(7374038753477564581)
XLA Ops:
  0.0 0.0 copy-start
  0.0 0.0 copy-start.1
  0.0 1.1 %copy-done.1 = f32[64,2048]{1,0:T(8,128)S(1)} copy-done((f32[64,2048]{1,0:T(8,128)S(1)}, f32[64,2048]{1,0:T(8,128)}, u32[]{:S(2)}) %copy-start.1) | copy-done | bytes 524312
  1.1 0.9 %whiten.1 = (bf16[16,8,8,128]{3,2,1,0:T(8,128)(2,1)}, bf16[1024,128]{1,0:T(8,128)(2,1)S(1)}) custom-call(f32[64,2048]{1,0:T(8,128)S(1)} %copy-done.1), custom_call_target="tpu_custom_call" | custom-call | tf_op jit(solution)/shard_map/whiten/pallas_call | solution.py:37
  1.9 11.5 %all-to-all-start = ((bf16[128,8,128]{2,1,0:T(8,128)(2,1)}), bf16[128,8,128]{2,1,0:T(8,128)(2,1)S(1)}, u32[]{:S(2)}, u32[]{:S(2)}) async-start(bf16[128,8,128]{2,1,0:T(8,128)(2,1)} %bitcast.3), calls=%async_computation | async-start | bytes 524288 | tf_op jit(solution)/shard_map/all_to_all | solution.py:161
  13.4 1.4 %collective-permute-start = (bf16[1024,128]{1,0:T(8,128)(2,1)S(1)}, bf16[1024,128]{1,0:T(8,128)(2,1)S(1)}, u32[]{:S(2)}, u32[]{:S(2)}) collective-permute-start(bf16[1024,128]{1,0:T(8,128)(2,1)S(1)} %get-tuple-element.7), channel_id=1, source_target_pairs={{0,1},{1,0},{2,3},{3,2},{4,5},{5,4},{6,7},{7,6},{8,9},{9,8},{10,11... | collective-permute-start | bytes 786440 | tf_op jit(solution)/shard_map/ppermute | solution.py:162
  14.8 9.6 %all-to-all-done = bf16[128,8,128]{2,1,0:T(8,128)(2,1)S(1)} async-done(((bf16[128,8,128]{2,1,0:T(8,128)(2,1)}), bf16[128,8,128]{2,1,0:T(8,128)(2,1)S(1)}, u32[]{:S(2)}, u32[]{:S(2)}) %all-to-all-start) | async-done | bytes 262176 | tf_op jit(solution)/shard_map/all_to_all | solution.py:161
  24.4 0.0 copy-start.2
  24.4 0.7 copy-done.2
  25.1 1.5 %choose.1 = bf16[16,3,8,8,128]{4,3,2,1,0:T(8,128)(2,1)} custom-call(s32[3,16]{1,0:T(4,128)S(1)} %copy-done.2, bf16[16,8,8,128]{3,2,1,0:T(8,128)(2,1)S(1)} %bitcast.5), custom_call_target="tpu_custom_call" | custom-call | tf_op jit(solution)/shard_map/choose/pallas_call | solution.py:55
  26.6 4.2 %all-to-all-start.1 = ((bf16[16,3,8,8,128]{4,3,2,1,0:T(8,128)(2,1)}), bf16[16,3,8,8,128]{4,3,2,1,0:T(8,128)(2,1)S(1)}, u32[]{:S(2)}, u32[]{:S(2)}) async-start(bf16[16,3,8,8,128]{4,3,2,1,0:T(8,128)(2,1)} %choose.1), calls=%async_computation.1 | async-start | bytes 1572864 | tf_op jit(solution)/shard_map/all_to_all | solution.py:168
  30.8 0.0 collective-permute-done
  30.8 0.1 pad_maximum_fusion.s0_ref
  30.9 0.8 %collective-permute-start.3 = (bf16[2,1024,128]{2,1,0:T(8,128)(2,1)S(1)}, bf16[2,1024,128]{2,1,0:T(8,128)(2,1)S(1)}, u32[]{:S(2)}, u32[]{:S(2)}) collective-permute-start(bf16[2,1024,128]{2,1,0:T(8,128)(2,1)S(1)} %pad_maximum_fusion.s0_ref), channel_id=1, source_target_pairs={{0,6},{1,7},{2,4},{3,5},{4,2},{5,3},{6,0},{7,1},{8,14},{9,15},{10,... | collective-permute-start | bytes 1572872 | tf_op jit(solution)/shard_map/ppermute | solution.py:166
  31.7 1.3 %collective-permute-start.2 = (bf16[2,1024,128]{2,1,0:T(8,128)(2,1)S(1)}, bf16[2,1024,128]{2,1,0:T(8,128)(2,1)S(1)}, u32[]{:S(2)}, u32[]{:S(2)}) collective-permute-start(bf16[2,1024,128]{2,1,0:T(8,128)(2,1)S(1)} %pad_maximum_fusion.s0_ref), channel_id=1, source_target_pairs={{0,4},{1,5},{2,6},{3,7},{4,0},{5,1},{6,2},{7,3},{8,12},{9,13},{10,... | collective-permute-start | bytes 1572872 | tf_op jit(solution)/shard_map/ppermute | solution.py:166
  33.0 1.2 %collective-permute-start.1 = (bf16[2,1024,128]{2,1,0:T(8,128)(2,1)S(1)}, bf16[2,1024,128]{2,1,0:T(8,128)(2,1)S(1)}, u32[]{:S(2)}, u32[]{:S(2)}) collective-permute-start(bf16[2,1024,128]{2,1,0:T(8,128)(2,1)S(1)} %pad_maximum_fusion.s0_ref), channel_id=1, source_target_pairs={{0,2},{1,3},{2,0},{3,1},{4,6},{5,7},{6,4},{7,5},{8,10},{9,11},{10,... | collective-permute-start | bytes 1572872 | tf_op jit(solution)/shard_map/ppermute | solution.py:166
  34.2 0.0 copy-done
  34.2 0.2 dynamic-slice_reduce_fusion
  34.4 0.1 pad_add_fusion.offs
  34.5 22.3 %collective-permute-done.3.s3_ref = bf16[2,1024,128]{2,1,0:T(8,128)(2,1)S(1)} collective-permute-done((bf16[2,1024,128]{2,1,0:T(8,128)(2,1)S(1)}, bf16[2,1024,128]{2,1,0:T(8,128)(2,1)S(1)}, u32[]{:S(2)}, u32[]{:S(2)}) %collective-permute-start.3) | collective-permute-done | bytes 524320 | tf_op jit(solution)/shard_map/ppermute | solution.py:166
  56.8 0.0 collective-permute-done.2.s2_ref
  56.8 0.3 collective-permute-done.1.s1_ref
  57.1 0.0 all-to-all-done.1.t_ref
  57.1 16.9 %corr.1 = f32[8,3,64,256]{3,2,1,0:T(8,128)} custom-call(s32[4]{0:T(128)S(1)} %pad_add_fusion.offs, bf16[2,1024,128]{2,1,0:T(8,128)(2,1)S(1)} %pad_maximum_fusion.s0_ref, bf16[2,1024,128]{2,1,0:T(8,128)(2,1)S(1)} %collective-permute-done.1.s1_ref, bf16[2,1024,128]{2,1,0:T(8,128)(2,1)S(1)} %collective-permute-done.2.s2_ref, ...), custom_call_target="tpu_custom_call" | custom-call | tf_op jit(solution)/shard_map/corr/pallas_call | solution.py:143
Async XLA Ops:
  0.0 34.2 %copy-start = (s32[3,16]{1,0:T(4,128)S(1)}, s32[3,16]{1,0:T(4,128)}, u32[]{:S(2)}) copy-start(s32[3,16]{1,0:T(4,128)} %param.5) | copy-start | bytes 580
  0.0 1.1 %copy-start.1 = (f32[64,2048]{1,0:T(8,128)S(1)}, f32[64,2048]{1,0:T(8,128)}, u32[]{:S(2)}) copy-start(f32[64,2048]{1,0:T(8,128)} %x_ref.1) | copy-start | bytes 1572868
  1.9 22.5 %all-to-all-start = ((bf16[128,8,128]{2,1,0:T(8,128)(2,1)}), bf16[128,8,128]{2,1,0:T(8,128)(2,1)S(1)}, u32[]{:S(2)}, u32[]{:S(2)}) async-start(bf16[128,8,128]{2,1,0:T(8,128)(2,1)} %bitcast.3), calls=%async_computation | async-start | bytes 524288 | tf_op jit(solution)/shard_map/all_to_all | solution.py:161
  13.4 17.4 %collective-permute-start = (bf16[1024,128]{1,0:T(8,128)(2,1)S(1)}, bf16[1024,128]{1,0:T(8,128)(2,1)S(1)}, u32[]{:S(2)}, u32[]{:S(2)}) collective-permute-start(bf16[1024,128]{1,0:T(8,128)(2,1)S(1)} %get-tuple-element.7), channel_id=1, source_target_pairs={{0,1},{1,0},{2,3},{3,2},{4,5},{5,4},{6,7},{7,6},{8,9},{9,8},{10,11... | collective-permute-start | bytes 786440 | tf_op jit(solution)/shard_map/ppermute | solution.py:162
  24.4 0.7 copy-start.2
  26.6 30.5 %all-to-all-start.1 = ((bf16[16,3,8,8,128]{4,3,2,1,0:T(8,128)(2,1)}), bf16[16,3,8,8,128]{4,3,2,1,0:T(8,128)(2,1)S(1)}, u32[]{:S(2)}, u32[]{:S(2)}) async-start(bf16[16,3,8,8,128]{4,3,2,1,0:T(8,128)(2,1)} %choose.1), calls=%async_computation.1 | async-start | bytes 1572864 | tf_op jit(solution)/shard_map/all_to_all | solution.py:168
  30.9 25.9 %collective-permute-start.3 = (bf16[2,1024,128]{2,1,0:T(8,128)(2,1)S(1)}, bf16[2,1024,128]{2,1,0:T(8,128)(2,1)S(1)}, u32[]{:S(2)}, u32[]{:S(2)}) collective-permute-start(bf16[2,1024,128]{2,1,0:T(8,128)(2,1)S(1)} %pad_maximum_fusion.s0_ref), channel_id=1, source_target_pairs={{0,6},{1,7},{2,4},{3,5},{4,2},{5,3},{6,0},{7,1},{8,14},{9,15},{10,... | collective-permute-start | bytes 1572872 | tf_op jit(solution)/shard_map/ppermute | solution.py:166
  31.7 25.1 %collective-permute-start.2 = (bf16[2,1024,128]{2,1,0:T(8,128)(2,1)S(1)}, bf16[2,1024,128]{2,1,0:T(8,128)(2,1)S(1)}, u32[]{:S(2)}, u32[]{:S(2)}) collective-permute-start(bf16[2,1024,128]{2,1,0:T(8,128)(2,1)S(1)} %pad_maximum_fusion.s0_ref), channel_id=1, source_target_pairs={{0,4},{1,5},{2,6},{3,7},{4,0},{5,1},{6,2},{7,3},{8,12},{9,13},{10,... | collective-permute-start | bytes 1572872 | tf_op jit(solution)/shard_map/ppermute | solution.py:166
  33.0 24.1 %collective-permute-start.1 = (bf16[2,1024,128]{2,1,0:T(8,128)(2,1)S(1)}, bf16[2,1024,128]{2,1,0:T(8,128)(2,1)S(1)}, u32[]{:S(2)}, u32[]{:S(2)}) collective-permute-start(bf16[2,1024,128]{2,1,0:T(8,128)(2,1)S(1)} %pad_maximum_fusion.s0_ref), channel_id=1, source_target_pairs={{0,2},{1,3},{2,0},{3,1},{4,6},{5,7},{6,4},{7,5},{8,10},{9,11},{10,... | collective-permute-start | bytes 1572872 | tf_op jit(solution)/shard_map/ppermute | solution.py:166
where the time goes:
time: 74.3 us; the launch traced here: 74 us
  waiting for transfers between devices  32.2 us (43%)
  starting transfers between devices  20.5 us (28%)
  Pallas kernels  19.3 us (26%)
  local copies, waits for them, and re-layouts  1.92 us (3%)
    ppermute x3, waiting for transfers between devices, local(): far.append(lax.ppermute(pair, 'win', [(i, i ^ 2 * r) for i in range(WINS)]))  22.6 us
    pallas_call x1, Pallas kernels, corr(): pl.pallas_call(corr_kernel, out_shape=jax.ShapeDtypeStruct((ROWS, MATCH,...  16.9 us
    all_to_all x1, starting transfers between devices, local(): lax.all_to_all(cut.reshape(BLOCKS * WINS, ROWS, 128), ('chan', 'win'), 0, 0)  11.5 us
    all_to_all x1, waiting for transfers between devices, local(): lax.all_to_all(cut.reshape(BLOCKS * WINS, ROWS, 128), ('chan', 'win'), 0, 0)  9.58 us
    all_to_all x1, starting transfers between devices, local(): partner = lax.all_to_all(sent, 'chan', 0, 0)  4.2 us
    ppermute x3, starting transfers between devices, local(): far.append(lax.ppermute(pair, 'win', [(i, i ^ 2 * r) for i in range(WINS)]))  3.33 us
    unnamed x6, local copies, waits for them, and re-layouts  1.74 us
    pallas_call x1, Pallas kernels, choose(): pl.pallas_call(choose_kernel, out_shape=jax.ShapeDtypeStruct((BLOCKS, MAT...  1.5 us
  transfers between devices with their start and end apart: 6, of which 3 were waited for; matrix products, arithmetic and copies ran while one was open for 0% of the time, Pallas kernels for 2%

commit v1 on v0

--- a/solution.py
+++ b/solution.py
@@ -19,6 +19,7 @@
 WIDE = LEN + 512
 PAD = 96
 PAIR = 2
+NEAR = (SPAN // 128 + 1) // 2
 SCALE = 1.0 / 128.0
 
 
@@ -61,81 +62,101 @@
     )(matchings, chunks)
 
 
-def corr_kernel(offs, s0_ref, s1_ref, s2_ref, s3_ref, t_ref, o_ref, y0, y1, ts0, ts1, acc):
+def corr_kernel(offs, s0_ref, s1_ref, s2_ref, s3_ref, t_ref, o_ref, y0, y1, v0, v1, e0, e1, d0, d1, t0, t1, acc):
     lane = lax.broadcasted_iota(jnp.int32, (1, 128), 1)
     mine = offs[MATCH]
     sources = (s0_ref, s1_ref, s2_ref, s3_ref)
 
-    def source(r, y):
+    def source(r, y, v):
         for n in range(PAIR):
             x = sources[r][n].astype(jnp.float32)
             swapped = pltpu.roll(x, CHANS, 1)
             gap = jnp.zeros((FINE, 128), jnp.float32)
             now = jnp.concatenate([x, swapped, gap], axis=0)
             late = jnp.concatenate([gap, swapped, x], axis=0)
-            y[n, PAD:PAD + LEN + FINE, :] = jnp.where(lane < CHANS, now, late).astype(jnp.bfloat16)
-
-    def partner(r, ts):
+            both = jnp.where(lane < CHANS, now, late)
+            y[n, PAD:PAD + LEN + FINE, :] = both.astype(jnp.bfloat16)
+            v[n, PAD:PAD + LEN + FINE - 128, :] = (both[:-128] + both[128:]).astype(jnp.bfloat16)
+            v[n, :PAD, :] = both[128 - PAD:128].astype(jnp.bfloat16)
+
+    def partner(r, even, odd, late):
         zeros = jnp.zeros((ROWS, 256), jnp.float32)
         for n in range(PAIR):
             w = lax.bitwise_xor(mine, 2 * r + n)
             for m in range(MATCH):
                 cut = [t_ref[c, m, w].astype(jnp.float32) for c in range(BLOCKS)]
                 row = jnp.concatenate([zeros] + cut + [zeros], axis=1)
-                even = pltpu.roll(row, WIDE - 128 - offs[m], 1)
-                odd = pltpu.roll(even, WIDE - 1, 1)
-                both = jnp.concatenate([even, odd], axis=0).astype(jnp.bfloat16)
+                now = pltpu.roll(row, WIDE - 128 - offs[m], 1)
+                both = jnp.concatenate([now, pltpu.roll(now, WIDE - 1, 1)], axis=0)
+                change = (both[:, :WIDE - 128] - both[:, 128:]).astype(jnp.bfloat16)
+                both = both.astype(jnp.bfloat16)
                 for k in range(FINE // 2):
-                    first = 128 * m + 16 * k
-                    ts[n, first:first + 16, :] = both[:, 2 * k:2 * k + SPAN + 128]
-
-    def product(y, ts, fresh):
-        lhs = jnp.concatenate(
-            [
-                jnp.concatenate([ts[n, :, 128 * top:128 * top + SPAN] for n in range(PAIR)], axis=1)
-                for top in range(2)
-            ],
-            axis=0,
-        )
-        rhs = jnp.concatenate(
-            [
-                jnp.concatenate([y[n, PAD - 2 * FINE * q:PAD - 2 * FINE * q + SPAN, :] for n in range(PAIR)], axis=0)
-                for q in range(GROUPS // 2)
-            ],
-            axis=1,
-        )
-        r = jnp.dot(lhs, rhs, preferred_element_type=jnp.float32)
-        for q in range(GROUPS // 2):
-            part = r[:, 128 * q:128 * (q + 1)]
-            acc[q] = part if fresh else acc[q] + part
+                    rows = pl.ds(128 * m + 16 * k, 16)
+
+                    def shifted(p, block):
+                        one = p[:, 128 * block:128 * (block + 1)]
+                        if k == 0:
+                            return one
+                        return pltpu.roll(jnp.where(lane >= 2 * k, one, p[:, 128 * (block + 1):128 * (block + 2)]), 128 - 2 * k, 1)
+
+                    for i in range(NEAR):
+                        first = 128 * (n * NEAR + i)
+                        even[rows, first:first + 128] = shifted(change, 2 * i)
+                        late[rows, first:first + 128] = shifted(both, 2 * i + 1)
+                    for i in range(NEAR - 1):
+                        first = 128 * (n * (NEAR - 1) + i)
+                        odd[rows, first:first + 128] = shifted(change, 2 * i + 1)
+
+    def product(y, v, even, odd, late, fresh):
+        def blocks(pick):
+            return jnp.concatenate(
+                [
+                    jnp.concatenate([ref[n, pl.ds(PAD - 2 * FINE * q + 128 * i, 128), :] for n in range(PAIR) for ref, i in pick], axis=0)
+                    for q in range(GROUPS // 2)
+                ],
+                axis=1,
+            )
+
+        near = [(y, 2 * i) for i in range(NEAR)]
+        far = [(y, 2 * i + 1) for i in range(NEAR - 1)]
+        sums = [(v, 2 * i) for i in range(NEAR - 1)] + [(y, 2 * NEAR - 2)]
+        for j, (lhs, pick) in enumerate(((even, near), (late, sums), (odd, far))):
+            r = jnp.dot(lhs[...], blocks(pick), preferred_element_type=jnp.float32)
+            for q in range(GROUPS // 2):
+                part = r[:, 128 * q:128 * (q + 1)]
+                acc[j, q] = part if fresh else acc[j, q] + part
 
     for y in (y0, y1):
         for n in range(PAIR):
             y[n, :PAD, :] = jnp.zeros((PAD, 128), jnp.bfloat16)
             y[n, PAD + LEN + FINE:, :] = jnp.zeros((SPAN - LEN - FINE, 128), jnp.bfloat16)
-    buffers = ((y0, ts0), (y1, ts1))
     rounds = WINS // PAIR
-    source(0, y0)
-    partner(0, ts0)
+    buffers = ((y0, v0, e0, d0, t0), (y1, v1, e1, d1, t1))
+    source(0, *buffers[0][:2])
+    partner(0, *buffers[0][2:])
     for r in range(rounds):
         if r + 1 < rounds:
-            source(r + 1, buffers[(r + 1) % 2][0])
-            partner(r + 1, buffers[(r + 1) % 2][1])
+            source(r + 1, *buffers[(r + 1) % 2][:2])
+            partner(r + 1, *buffers[(r + 1) % 2][2:])
         product(*buffers[r % 2], r == 0)
 
-    for top in range(2):
+    for top, sign, j in ((0, 1, 0), (1, -1, 2)):
+        lanes = pl.ds(128 * top, 128)
         for m in range(MATCH):
             for b in range(0, ROWS, 2):
-                base = (top * MATCH + m) * 128 + b
+
+                def lags(q, row):
+                    rows = pl.ds(128 * m + row, FINE, stride=ROWS)
+                    return (acc[1, q, rows, :] + sign * acc[j, q, rows, :]) * SCALE
+
                 rows = []
                 for q in range(GROUPS // 2):
-                    lo = acc[q, pl.ds(base, FINE, stride=ROWS), :] * SCALE
-                    hi = acc[q, pl.ds(base + 1, FINE, stride=ROWS), :] * SCALE
+                    lo, hi = lags(q, b), lags(q, b + 1)
                     rows.append(jnp.where(lane < CHANS, lo, pltpu.roll(hi, CHANS, 1)))
                     rows.append(jnp.where(lane < CHANS, pltpu.roll(lo, CHANS, 1), hi))
                 z = jnp.concatenate(rows, axis=0).T
-                o_ref[b, m, :, 128 * top:128 * (top + 1)] = z[:CHANS]
-                o_ref[b + 1, m, :, 128 * top:128 * (top + 1)] = z[CHANS:]
+                o_ref[b, m, :, lanes] = z[:CHANS]
+                o_ref[b + 1, m, :, lanes] = z[CHANS:]
 
 
 def corr(offs, sources, partner):
@@ -146,9 +167,12 @@
         in_specs=[pl.BlockSpec(memory_space=pltpu.SMEM)] + [vmem] * 5,
         out_specs=vmem,
         scratch_shapes=[pltpu.VMEM((PAIR, PAD + SPAN, 128), jnp.bfloat16)] * 2
-        + [pltpu.VMEM((PAIR, MATCH * FINE * ROWS, SPAN + 128), jnp.bfloat16)] * 2
-        + [pltpu.VMEM((GROUPS // 2, 2 * MATCH * FINE * ROWS, 128), jnp.float32)],
-        compiler_params=pltpu.CompilerParams(vmem_limit_bytes=28 << 20),
+        + [pltpu.VMEM((PAIR, PAD + LEN + FINE - 128, 128), jnp.bfloat16)] * 2
+        + [pltpu.VMEM((MATCH * FINE * ROWS, PAIR * NEAR * 128), jnp.bfloat16)] * 2
+        + [pltpu.VMEM((MATCH * FINE * ROWS, PAIR * (NEAR - 1) * 128), jnp.bfloat16)] * 2
+        + [pltpu.VMEM((MATCH * FINE * ROWS, PAIR * NEAR * 128), jnp.bfloat16)] * 2
+        + [pltpu.VMEM((3, GROUPS // 2, MATCH * FINE * ROWS, 128), jnp.float32)],
+        compiler_params=pltpu.CompilerParams(vmem_limit_bytes=36 << 20),
         name="corr",
     )(offs, *sources, partner)
 

time: 74.3 us -> 71.9 us (0.968)
  Pallas kernels: 19.3 us -> 16.8 us
    pallas_call x1, Pallas kernels: 16.9 us -> 14.5 us  [corr(): pl.pallas_call(corr_kernel, out_shape=jax.ShapeDtypeStruct((ROWS, MATCH,...]
where the time goes in v1:
time: 71.9 us; the launch traced here: 71.6 us
  waiting for transfers between devices  32.2 us (45%)
  starting transfers between devices  20.5 us (29%)
  Pallas kernels  16.8 us (23%)
  local copies, waits for them, and re-layouts  1.92 us (3%)
    ppermute x3, waiting for transfers between devices, local(): far.append(lax.ppermute(pair, 'win', [(i, i ^ 2 * r) for i in range(WINS)]))  22.6 us
    pallas_call x1, Pallas kernels, corr(): pl.pallas_call(corr_kernel, out_shape=jax.ShapeDtypeStruct((ROWS, MATCH,...  14.5 us
    all_to_all x1, starting transfers between devices, local(): lax.all_to_all(cut.reshape(BLOCKS * WINS, ROWS, 128), ('chan', 'win'), 0, 0)  11.5 us
    all_to_all x1, waiting for transfers between devices, local(): lax.all_to_all(cut.reshape(BLOCKS * WINS, ROWS, 128), ('chan', 'win'), 0, 0)  9.58 us
    all_to_all x1, starting transfers between devices, local(): partner = lax.all_to_all(sent, 'chan', 0, 0)  4.2 us
    ppermute x3, starting transfers between devices, local(): far.append(lax.ppermute(pair, 'win', [(i, i ^ 2 * r) for i in range(WINS)]))  3.33 us
    unnamed x6, local copies, waits for them, and re-layouts  1.74 us
    pallas_call x1, Pallas kernels, choose(): pl.pallas_call(choose_kernel, out_shape=jax.ShapeDtypeStruct((BLOCKS, MAT...  1.5 us
  transfers between devices with their start and end apart: 6, of which 3 were waited for; matrix products, arithmetic and copies ran while one was open for 0% of the time, Pallas kernels for 2%

profile of v1, /device:TPU:1, one launch (start us, length us, event | category | flops | bytes accessed | tf_op | source)
XLA Modules:
  0.0 71.6 jit_solution(12457969892605483915)
XLA Ops:
  0.0 0.0 copy-start
  0.0 0.0 copy-start.1
  0.0 1.1 %copy-done.1 = f32[64,2048]{1,0:T(8,128)S(1)} copy-done((f32[64,2048]{1,0:T(8,128)S(1)}, f32[64,2048]{1,0:T(8,128)}, u32[]{:S(2)}) %copy-start.1) | copy-done | bytes 524312
  1.1 0.9 %whiten.1 = (bf16[16,8,8,128]{3,2,1,0:T(8,128)(2,1)}, bf16[1024,128]{1,0:T(8,128)(2,1)S(1)}) custom-call(f32[64,2048]{1,0:T(8,128)S(1)} %copy-done.1), custom_call_target="tpu_custom_call" | custom-call | tf_op jit(solution)/shard_map/whiten/pallas_call | solution.py:38
  1.9 11.5 %all-to-all-start = ((bf16[128,8,128]{2,1,0:T(8,128)(2,1)}), bf16[128,8,128]{2,1,0:T(8,128)(2,1)S(1)}, u32[]{:S(2)}, u32[]{:S(2)}) async-start(bf16[128,8,128]{2,1,0:T(8,128)(2,1)} %bitcast.3), calls=%async_computation | async-start | bytes 524288 | tf_op jit(solution)/shard_map/all_to_all | solution.py:185
  13.4 1.4 %collective-permute-start = (bf16[1024,128]{1,0:T(8,128)(2,1)S(1)}, bf16[1024,128]{1,0:T(8,128)(2,1)S(1)}, u32[]{:S(2)}, u32[]{:S(2)}) collective-permute-start(bf16[1024,128]{1,0:T(8,128)(2,1)S(1)} %get-tuple-element.7), channel_id=1, source_target_pairs={{0,1},{1,0},{2,3},{3,2},{4,5},{5,4},{6,7},{7,6},{8,9},{9,8},{10,11... | collective-permute-start | bytes 786440 | tf_op jit(solution)/shard_map/ppermute | solution.py:186
  14.8 9.6 %all-to-all-done = bf16[128,8,128]{2,1,0:T(8,128)(2,1)S(1)} async-done(((bf16[128,8,128]{2,1,0:T(8,128)(2,1)}), bf16[128,8,128]{2,1,0:T(8,128)(2,1)S(1)}, u32[]{:S(2)}, u32[]{:S(2)}) %all-to-all-start) | async-done | bytes 262176 | tf_op jit(solution)/shard_map/all_to_all | solution.py:185
  24.4 0.0 copy-start.2
  24.4 0.7 copy-done.2
  25.1 1.5 %choose.1 = bf16[16,3,8,8,128]{4,3,2,1,0:T(8,128)(2,1)} custom-call(s32[3,16]{1,0:T(4,128)S(1)} %copy-done.2, bf16[16,8,8,128]{3,2,1,0:T(8,128)(2,1)S(1)} %bitcast.5), custom_call_target="tpu_custom_call" | custom-call | tf_op jit(solution)/shard_map/choose/pallas_call | solution.py:56
  26.6 4.2 %all-to-all-start.1 = ((bf16[16,3,8,8,128]{4,3,2,1,0:T(8,128)(2,1)}), bf16[16,3,8,8,128]{4,3,2,1,0:T(8,128)(2,1)S(1)}, u32[]{:S(2)}, u32[]{:S(2)}) async-start(bf16[16,3,8,8,128]{4,3,2,1,0:T(8,128)(2,1)} %choose.1), calls=%async_computation.1 | async-start | bytes 1572864 | tf_op jit(solution)/shard_map/all_to_all | solution.py:192
  30.8 0.0 collective-permute-done
  30.8 0.1 pad_maximum_fusion.s0_ref
  30.9 0.8 %collective-permute-start.3 = (bf16[2,1024,128]{2,1,0:T(8,128)(2,1)S(1)}, bf16[2,1024,128]{2,1,0:T(8,128)(2,1)S(1)}, u32[]{:S(2)}, u32[]{:S(2)}) collective-permute-start(bf16[2,1024,128]{2,1,0:T(8,128)(2,1)S(1)} %pad_maximum_fusion.s0_ref), channel_id=1, source_target_pairs={{0,6},{1,7},{2,4},{3,5},{4,2},{5,3},{6,0},{7,1},{8,14},{9,15},{10,... | collective-permute-start | bytes 1572872 | tf_op jit(solution)/shard_map/ppermute | solution.py:190
  31.7 1.3 %collective-permute-start.2 = (bf16[2,1024,128]{2,1,0:T(8,128)(2,1)S(1)}, bf16[2,1024,128]{2,1,0:T(8,128)(2,1)S(1)}, u32[]{:S(2)}, u32[]{:S(2)}) collective-permute-start(bf16[2,1024,128]{2,1,0:T(8,128)(2,1)S(1)} %pad_maximum_fusion.s0_ref), channel_id=1, source_target_pairs={{0,4},{1,5},{2,6},{3,7},{4,0},{5,1},{6,2},{7,3},{8,12},{9,13},{10,... | collective-permute-start | bytes 1572872 | tf_op jit(solution)/shard_map/ppermute | solution.py:190
  33.0 1.2 %collective-permute-start.1 = (bf16[2,1024,128]{2,1,0:T(8,128)(2,1)S(1)}, bf16[2,1024,128]{2,1,0:T(8,128)(2,1)S(1)}, u32[]{:S(2)}, u32[]{:S(2)}) collective-permute-start(bf16[2,1024,128]{2,1,0:T(8,128)(2,1)S(1)} %pad_maximum_fusion.s0_ref), channel_id=1, source_target_pairs={{0,2},{1,3},{2,0},{3,1},{4,6},{5,7},{6,4},{7,5},{8,10},{9,11},{10,... | collective-permute-start | bytes 1572872 | tf_op jit(solution)/shard_map/ppermute | solution.py:190
  34.2 0.0 copy-done
  34.2 0.2 dynamic-slice_reduce_fusion
  34.4 0.1 pad_add_fusion.offs
  34.5 22.3 %collective-permute-done.3.s3_ref = bf16[2,1024,128]{2,1,0:T(8,128)(2,1)S(1)} collective-permute-done((bf16[2,1024,128]{2,1,0:T(8,128)(2,1)S(1)}, bf16[2,1024,128]{2,1,0:T(8,128)(2,1)S(1)}, u32[]{:S(2)}, u32[]{:S(2)}) %collective-permute-start.3) | collective-permute-done | bytes 524320 | tf_op jit(solution)/shard_map/ppermute | solution.py:190
  56.8 0.0 collective-permute-done.2.s2_ref
  56.8 0.3 collective-permute-done.1.s1_ref
  57.1 0.0 all-to-all-done.1.t_ref
  57.1 14.5 %corr.1 = f32[8,3,64,256]{3,2,1,0:T(8,128)} custom-call(s32[4]{0:T(128)S(1)} %pad_add_fusion.offs, bf16[2,1024,128]{2,1,0:T(8,128)(2,1)S(1)} %pad_maximum_fusion.s0_ref, bf16[2,1024,128]{2,1,0:T(8,128)(2,1)S(1)} %collective-permute-done.1.s1_ref, bf16[2,1024,128]{2,1,0:T(8,128)(2,1)S(1)} %collective-permute-done.2.s2_ref, ...), custom_call_target="tpu_custom_call" | custom-call | tf_op jit(solution)/shard_map/corr/pallas_call | solution.py:164
Async XLA Ops:
  0.0 34.2 %copy-start = (s32[3,16]{1,0:T(4,128)S(1)}, s32[3,16]{1,0:T(4,128)}, u32[]{:S(2)}) copy-start(s32[3,16]{1,0:T(4,128)} %param.5) | copy-start | bytes 580
  0.0 1.1 %copy-start.1 = (f32[64,2048]{1,0:T(8,128)S(1)}, f32[64,2048]{1,0:T(8,128)}, u32[]{:S(2)}) copy-start(f32[64,2048]{1,0:T(8,128)} %x_ref.1) | copy-start | bytes 1572868
  1.9 22.5 %all-to-all-start = ((bf16[128,8,128]{2,1,0:T(8,128)(2,1)}), bf16[128,8,128]{2,1,0:T(8,128)(2,1)S(1)}, u32[]{:S(2)}, u32[]{:S(2)}) async-start(bf16[128,8,128]{2,1,0:T(8,128)(2,1)} %bitcast.3), calls=%async_computation | async-start | bytes 524288 | tf_op jit(solution)/shard_map/all_to_all | solution.py:185
  13.4 17.4 %collective-permute-start = (bf16[1024,128]{1,0:T(8,128)(2,1)S(1)}, bf16[1024,128]{1,0:T(8,128)(2,1)S(1)}, u32[]{:S(2)}, u32[]{:S(2)}) collective-permute-start(bf16[1024,128]{1,0:T(8,128)(2,1)S(1)} %get-tuple-element.7), channel_id=1, source_target_pairs={{0,1},{1,0},{2,3},{3,2},{4,5},{5,4},{6,7},{7,6},{8,9},{9,8},{10,11... | collective-permute-start | bytes 786440 | tf_op jit(solution)/shard_map/ppermute | solution.py:186
  24.4 0.7 copy-start.2
  26.6 30.5 %all-to-all-start.1 = ((bf16[16,3,8,8,128]{4,3,2,1,0:T(8,128)(2,1)}), bf16[16,3,8,8,128]{4,3,2,1,0:T(8,128)(2,1)S(1)}, u32[]{:S(2)}, u32[]{:S(2)}) async-start(bf16[16,3,8,8,128]{4,3,2,1,0:T(8,128)(2,1)} %choose.1), calls=%async_computation.1 | async-start | bytes 1572864 | tf_op jit(solution)/shard_map/all_to_all | solution.py:192
  30.9 25.9 %collective-permute-start.3 = (bf16[2,1024,128]{2,1,0:T(8,128)(2,1)S(1)}, bf16[2,1024,128]{2,1,0:T(8,128)(2,1)S(1)}, u32[]{:S(2)}, u32[]{:S(2)}) collective-permute-start(bf16[2,1024,128]{2,1,0:T(8,128)(2,1)S(1)} %pad_maximum_fusion.s0_ref), channel_id=1, source_target_pairs={{0,6},{1,7},{2,4},{3,5},{4,2},{5,3},{6,0},{7,1},{8,14},{9,15},{10,... | collective-permute-start | bytes 1572872 | tf_op jit(solution)/shard_map/ppermute | solution.py:190
  31.7 25.1 %collective-permute-start.2 = (bf16[2,1024,128]{2,1,0:T(8,128)(2,1)S(1)}, bf16[2,1024,128]{2,1,0:T(8,128)(2,1)S(1)}, u32[]{:S(2)}, u32[]{:S(2)}) collective-permute-start(bf16[2,1024,128]{2,1,0:T(8,128)(2,1)S(1)} %pad_maximum_fusion.s0_ref), channel_id=1, source_target_pairs={{0,4},{1,5},{2,6},{3,7},{4,0},{5,1},{6,2},{7,3},{8,12},{9,13},{10,... | collective-permute-start | bytes 1572872 | tf_op jit(solution)/shard_map/ppermute | solution.py:190
  33.0 24.1 %collective-permute-start.1 = (bf16[2,1024,128]{2,1,0:T(8,128)(2,1)S(1)}, bf16[2,1024,128]{2,1,0:T(8,128)(2,1)S(1)}, u32[]{:S(2)}, u32[]{:S(2)}) collective-permute-start(bf16[2,1024,128]{2,1,0:T(8,128)(2,1)S(1)} %pad_maximum_fusion.s0_ref), channel_id=1, source_target_pairs={{0,2},{1,3},{2,0},{3,1},{4,6},{5,7},{6,4},{7,5},{8,10},{9,11},{10,... | collective-permute-start | bytes 1572872 | tf_op jit(solution)/shard_map/ppermute | solution.py:190

commit v2 on v1

--- a/solution.py
+++ b/solution.py
@@ -23,24 +23,28 @@
 SCALE = 1.0 / 128.0
 
 
-def whiten_kernel(x_ref, cut_ref, turned_ref):
-    x = x_ref[...]
+def whitened(x):
     power = jnp.mean(x * x, axis=1, keepdims=True)
-    white = x / jnp.sqrt(power + 1e-06)
+    return x / jnp.sqrt(power + 1e-06)
+
+
+def cut_kernel(x_ref, cut_ref):
+    white = whitened(x_ref[...])
     for c in range(BLOCKS):
         for g in range(WINS):
             cut_ref[c, g] = white[g * ROWS:(g + 1) * ROWS, 128 * c:128 * (c + 1)].astype(jnp.bfloat16)
+
+
+def turn_kernel(x_ref, turned_ref):
+    white = whitened(x_ref[...])
     halves = jnp.concatenate([white[:, :HALF], white[:, HALF:]], axis=0)
     turned_ref[...] = halves.T.astype(jnp.bfloat16)
 
 
-def whiten(x):
+def whiten(kernel, shape, x):
     return pl.pallas_call(
-        whiten_kernel,
-        out_shape=(
-            jax.ShapeDtypeStruct((BLOCKS, WINS, ROWS, 128), jnp.bfloat16),
-            jax.ShapeDtypeStruct((HALF, 128), jnp.bfloat16),
-        ),
+        kernel,
+        out_shape=jax.ShapeDtypeStruct(shape, jnp.bfloat16),
         compiler_params=pltpu.CompilerParams(vmem_limit_bytes=4 << 20),
         name="whiten",
     )(x)
@@ -62,14 +66,14 @@
     )(matchings, chunks)
 
 
-def corr_kernel(offs, s0_ref, s1_ref, s2_ref, s3_ref, t_ref, o_ref, y0, y1, v0, v1, e0, e1, d0, d1, t0, t1, acc):
+def corr_kernel(offs, s0_ref, s1_ref, s2_ref, s3_ref, s4_ref, s5_ref, s6_ref, s7_ref, t_ref, o_ref, y0, y1, v0, v1, e0, e1, d0, d1, t0, t1, acc):
     lane = lax.broadcasted_iota(jnp.int32, (1, 128), 1)
     mine = offs[MATCH]
-    sources = (s0_ref, s1_ref, s2_ref, s3_ref)
+    sources = (s0_ref, s1_ref, s2_ref, s3_ref, s4_ref, s5_ref, s6_ref, s7_ref)
 
     def source(r, y, v):
         for n in range(PAIR):
-            x = sources[r][n].astype(jnp.float32)
+            x = sources[PAIR * r + n][...].astype(jnp.float32)
             swapped = pltpu.roll(x, CHANS, 1)
             gap = jnp.zeros((FINE, 128), jnp.float32)
             now = jnp.concatenate([x, swapped, gap], axis=0)
@@ -164,7 +168,7 @@
     return pl.pallas_call(
         corr_kernel,
         out_shape=jax.ShapeDtypeStruct((ROWS, MATCH, CHANS, LAGS), jnp.float32),
-        in_specs=[pl.BlockSpec(memory_space=pltpu.SMEM)] + [vmem] * 5,
+        in_specs=[pl.BlockSpec(memory_space=pltpu.SMEM)] + [vmem] * (WINS + 1),
         out_specs=vmem,
         scratch_shapes=[pltpu.VMEM((PAIR, PAD + SPAN, 128), jnp.bfloat16)] * 2
         + [pltpu.VMEM((PAIR, PAD + LEN + FINE - 128, 128), jnp.bfloat16)] * 2
@@ -181,16 +185,22 @@
     win = lax.axis_index("win")
     offs = lax.dynamic_index_in_dim(lag_offset, lax.axis_index("chan"), 1, keepdims=False)
     offs = jnp.concatenate([offs, jnp.full((1,), win, jnp.int32)])
-    cut, turned = whiten(waves)
+    cut = whiten(cut_kernel, (BLOCKS, WINS, ROWS, 128), waves)
     chunks = lax.all_to_all(cut.reshape(BLOCKS * WINS, ROWS, 128), ("chan", "win"), 0, 0)
-    other = lax.ppermute(turned, "win", [(i, i ^ 1) for i in range(WINS)])
-    pair = jnp.stack([turned, other])
-    far = []
+
+    def sent_to(piece, flip):
+        return lax.ppermute(piece, "win", [(i, i ^ flip) for i in range(WINS)])
+
+    turned = whiten(turn_kernel, (HALF, 128), waves)
+    other = sent_to(turned, 1)
+    sources = [turned, other]
     for r in (1, 2, 3):
-        far.append(lax.ppermute(pair, "win", [(i, i ^ (2 * r)) for i in range(WINS)]))
-    sent = choose(matchings, chunks.reshape(BLOCKS, WINS, ROWS, 128))
+        sources.append(sent_to(turned, 2 * r))
+        sources.append(sent_to(other, 2 * r))
+    table = jnp.clip(matchings, 0, BLOCKS - 1)
+    sent = choose(table, chunks.reshape(BLOCKS, WINS, ROWS, 128))
     partner = lax.all_to_all(sent, "chan", 0, 0)
-    return corr(offs, [pair] + far, partner)
+    return corr(offs, sources, partner)
 
 
 def solution(mesh):

time: 71.9 us -> 75 us (1.043)
  starting transfers between devices: 20.5 us -> 22.4 us
    ppermute x4 -> x7, starting transfers between devices: 4.77 us -> 6.67 us  [sent_to(): return lax.ppermute(piece, 'win', [(i, i ^ flip) for i in range(WINS)])]
    ppermute x4 -> x7, waiting for transfers between devices: 22.6 us -> 22.4 us  [sent_to(): return lax.ppermute(piece, 'win', [(i, i ^ flip) for i in range(WINS)])]
  transfers between devices with their start and end apart: 6 -> 9, of which waited for: 3 -> 4; matrix products, arithmetic and copies ran while one was open for 0% -> 1% of each run, Pallas kernels for 2% -> 0%
where the time goes in v2:
time: 75 us; the launch traced here: 74.2 us
  waiting for transfers between devices  32.7 us (44%)
  starting transfers between devices  22.4 us (30%)
  Pallas kernels  17.1 us (23%)
  local copies, waits for them, and re-layouts  1.25 us (2%)
  other arithmetic  0.77 us (1%)
    ppermute x7, waiting for transfers between devices, sent_to(): return lax.ppermute(piece, 'win', [(i, i ^ flip) for i in range(WINS)])  22.4 us
    pallas_call x1, Pallas kernels, corr(): pl.pallas_call(corr_kernel, out_shape=jax.ShapeDtypeStruct((ROWS, MATCH,...  14.5 us
    all_to_all x1, starting transfers between devices, local(): lax.all_to_all(cut.reshape(BLOCKS * WINS, ROWS, 128), ('chan', 'win'), 0, 0)  11.5 us
    all_to_all x1, waiting for transfers between devices, local(): lax.all_to_all(cut.reshape(BLOCKS * WINS, ROWS, 128), ('chan', 'win'), 0, 0)  10.3 us
    ppermute x7, starting transfers between devices, sent_to(): return lax.ppermute(piece, 'win', [(i, i ^ flip) for i in range(WINS)])  6.67 us
    all_to_all x1, starting transfers between devices, local(): partner = lax.all_to_all(sent, 'chan', 0, 0)  4.2 us
  transfers between devices with their start and end apart: 9, of which 4 were waited for; matrix products, arithmetic and copies ran while one was open for 1% of the time, Pallas kernels for 0%

profile of v2, /device:TPU:1, one launch (start us, length us, event | category | flops | bytes accessed | tf_op | source)
XLA Modules:
  0.0 74.2 jit_solution(1491558439725113925)
XLA Ops:
  0.0 0.0 copy-start
  0.0 0.0 copy-start.1
  0.0 1.1 %copy-done.1 = f32[64,2048]{1,0:T(8,128)S(1)} copy-done((f32[64,2048]{1,0:T(8,128)S(1)}, f32[64,2048]{1,0:T(8,128)}, u32[]{:S(2)}) %copy-start.1) | copy-done | bytes 524312
  1.1 0.9 %whiten.3 = bf16[16,8,8,128]{3,2,1,0:T(8,128)(2,1)} custom-call(f32[64,2048]{1,0:T(8,128)S(1)} %copy-done.1), custom_call_target="tpu_custom_call" | custom-call | tf_op jit(solution)/shard_map/whiten/pallas_call | solution.py:45
  1.9 0.0 copy-start.2
  1.9 11.5 %all-to-all-start = ((bf16[128,8,128]{2,1,0:T(8,128)(2,1)}), bf16[128,8,128]{2,1,0:T(8,128)(2,1)S(1)}, u32[]{:S(2)}, u32[]{:S(2)}) async-start(bf16[128,8,128]{2,1,0:T(8,128)(2,1)} %bitcast.1), calls=%async_computation | async-start | bytes 524288 | tf_op jit(solution)/shard_map/all_to_all | solution.py:189
  13.4 0.7 broadcast_clamp_fusion.match_ref
  14.1 10.3 %all-to-all-done = bf16[128,8,128]{2,1,0:T(8,128)(2,1)S(1)} async-done(((bf16[128,8,128]{2,1,0:T(8,128)(2,1)}), bf16[128,8,128]{2,1,0:T(8,128)(2,1)S(1)}, u32[]{:S(2)}, u32[]{:S(2)}) %all-to-all-start) | async-done | bytes 262176 | tf_op jit(solution)/shard_map/all_to_all | solution.py:189
  24.4 1.5 %choose.1 = bf16[16,3,8,8,128]{4,3,2,1,0:T(8,128)(2,1)} custom-call(s32[3,16]{1,0:T(4,128)S(1)} %broadcast_clamp_fusion.match_ref, bf16[16,8,8,128]{3,2,1,0:T(8,128)(2,1)S(1)} %bitcast.3), custom_call_target="tpu_custom_call" | custom-call | tf_op jit(solution)/shard_map/choose/pallas_call | solution.py:60
  25.9 4.2 %all-to-all-start.1 = ((bf16[16,3,8,8,128]{4,3,2,1,0:T(8,128)(2,1)}), bf16[16,3,8,8,128]{4,3,2,1,0:T(8,128)(2,1)S(1)}, u32[]{:S(2)}, u32[]{:S(2)}) async-start(bf16[16,3,8,8,128]{4,3,2,1,0:T(8,128)(2,1)} %choose.1), calls=%async_computation.1 | async-start | bytes 1572864 | tf_op jit(solution)/shard_map/all_to_all | solution.py:202
  30.1 0.0 copy-done.2
  30.1 0.3 whiten.2.s0_ref
  30.4 0.1 collective-permute-start
  30.5 1.2 %collective-permute-start.5 = (bf16[1024,128]{1,0:T(8,128)(2,1)S(1)}, bf16[1024,128]{1,0:T(8,128)(2,1)S(1)}, u32[]{:S(2)}, u32[]{:S(2)}) collective-permute-start(bf16[1024,128]{1,0:T(8,128)(2,1)S(1)} %whiten.2.s0_ref), channel_id=1, source_target_pairs={{0,6},{1,7},{2,4},{3,5},{4,2},{5,3},{6,0},{7,1},{8,14},{9,15},{10,... | collective-permute-start | bytes 786440 | tf_op jit(solution)/shard_map/ppermute | solution.py:192
  31.7 0.9 %collective-permute-start.3 = (bf16[1024,128]{1,0:T(8,128)(2,1)S(1)}, bf16[1024,128]{1,0:T(8,128)(2,1)S(1)}, u32[]{:S(2)}, u32[]{:S(2)}) collective-permute-start(bf16[1024,128]{1,0:T(8,128)(2,1)S(1)} %whiten.2.s0_ref), channel_id=1, source_target_pairs={{0,4},{1,5},{2,6},{3,7},{4,0},{5,1},{6,2},{7,3},{8,12},{9,13},{10,... | collective-permute-start | bytes 786440 | tf_op jit(solution)/shard_map/ppermute | solution.py:192
  32.6 1.2 %collective-permute-start.1 = (bf16[1024,128]{1,0:T(8,128)(2,1)S(1)}, bf16[1024,128]{1,0:T(8,128)(2,1)S(1)}, u32[]{:S(2)}, u32[]{:S(2)}) collective-permute-start(bf16[1024,128]{1,0:T(8,128)(2,1)S(1)} %whiten.2.s0_ref), channel_id=1, source_target_pairs={{0,2},{1,3},{2,0},{3,1},{4,6},{5,7},{6,4},{7,5},{8,10},{9,11},{10,... | collective-permute-start | bytes 786440 | tf_op jit(solution)/shard_map/ppermute | solution.py:192
  33.8 11.5 %collective-permute-done.s1_ref = bf16[1024,128]{1,0:T(8,128)(2,1)S(1)} collective-permute-done((bf16[1024,128]{1,0:T(8,128)(2,1)S(1)}, bf16[1024,128]{1,0:T(8,128)(2,1)S(1)}, u32[]{:S(2)}, u32[]{:S(2)}) %collective-permute-start) | collective-permute-done | bytes 262176 | tf_op jit(solution)/shard_map/ppermute | solution.py:192
  45.3 1.4 %collective-permute-start.6 = (bf16[1024,128]{1,0:T(8,128)(2,1)S(1)}, bf16[1024,128]{1,0:T(8,128)(2,1)S(1)}, u32[]{:S(2)}, u32[]{:S(2)}) collective-permute-start(bf16[1024,128]{1,0:T(8,128)(2,1)S(1)} %collective-permute-done.s1_ref), channel_id=1, source_target_pairs={{0,6},{1,7},{2,4},{3,5},{4,2},{5,3},{6,0},{7,1},{8,14},{9,15},{10,... | collective-permute-start | bytes 786440 | tf_op jit(solution)/shard_map/ppermute | solution.py:192
  46.7 0.7 collective-permute-start.4
  47.4 0.0 collective-permute-done.5.s6_ref
  47.4 1.2 %collective-permute-start.2 = (bf16[1024,128]{1,0:T(8,128)(2,1)S(1)}, bf16[1024,128]{1,0:T(8,128)(2,1)S(1)}, u32[]{:S(2)}, u32[]{:S(2)}) collective-permute-start(bf16[1024,128]{1,0:T(8,128)(2,1)S(1)} %collective-permute-done.s1_ref), channel_id=1, source_target_pairs={{0,2},{1,3},{2,0},{3,1},{4,6},{5,7},{6,4},{7,5},{8,10},{9,11},{10,... | collective-permute-start | bytes 786440 | tf_op jit(solution)/shard_map/ppermute | solution.py:192
  48.6 0.0 copy-done
  48.6 0.2 dynamic-slice_reduce_fusion
  48.8 0.1 pad_add_fusion.offs
  48.9 0.0 collective-permute-done.3.s4_ref
  48.9 0.0 collective-permute-done.1.s2_ref
  48.9 10.5 %collective-permute-done.6.s7_ref = bf16[1024,128]{1,0:T(8,128)(2,1)S(1)} collective-permute-done((bf16[1024,128]{1,0:T(8,128)(2,1)S(1)}, bf16[1024,128]{1,0:T(8,128)(2,1)S(1)}, u32[]{:S(2)}, u32[]{:S(2)}) %collective-permute-start.6) | collective-permute-done | bytes 262176 | tf_op jit(solution)/shard_map/ppermute | solution.py:192
  59.3 0.0 collective-permute-done.4.s5_ref
  59.3 0.4 collective-permute-done.2.s3_ref
  59.7 0.0 all-to-all-done.1.t_ref
  59.7 14.5 %corr.1 = f32[8,3,64,256]{3,2,1,0:T(8,128)} custom-call(s32[4]{0:T(128)S(1)} %pad_add_fusion.offs, bf16[1024,128]{1,0:T(8,128)(2,1)S(1)} %whiten.2.s0_ref, bf16[1024,128]{1,0:T(8,128)(2,1)S(1)} %collective-permute-done.s1_ref, bf16[1024,128]{1,0:T(8,128)(2,1)S(1)} %collective-permute-done.1.s2_ref, bf16[1024,128]{1,0:T(8,128)(2,1)S(1)} %collective-permute-done.2.s3_ref, ...), custom_call_target="tpu_custom_call" | custom-call | tf_op jit(solution)/shard_map/corr/pallas_call | solution.py:168
Async XLA Ops:
  0.0 48.6 %copy-start = (s32[3,16]{1,0:T(4,128)S(1)}, s32[3,16]{1,0:T(4,128)}, u32[]{:S(2)}) copy-start(s32[3,16]{1,0:T(4,128)} %param.5) | copy-start | bytes 580
  0.0 1.1 %copy-start.1 = (f32[64,2048]{1,0:T(8,128)S(1)}, f32[64,2048]{1,0:T(8,128)}, u32[]{:S(2)}) copy-start(f32[64,2048]{1,0:T(8,128)} %x_ref.3) | copy-start | bytes 1572868
  1.9 28.2 %copy-start.2 = (f32[64,2048]{1,0:T(8,128)S(1)}, f32[64,2048]{1,0:T(8,128)}, u32[]{:S(2)}) copy-start(f32[64,2048]{1,0:T(8,128)} %x_ref.3) | copy-start | bytes 1572868
  1.9 22.5 %all-to-all-start = ((bf16[128,8,128]{2,1,0:T(8,128)(2,1)}), bf16[128,8,128]{2,1,0:T(8,128)(2,1)S(1)}, u32[]{:S(2)}, u32[]{:S(2)}) async-start(bf16[128,8,128]{2,1,0:T(8,128)(2,1)} %bitcast.1), calls=%async_computation | async-start | bytes 524288 | tf_op jit(solution)/shard_map/all_to_all | solution.py:189
  25.9 33.8 %all-to-all-start.1 = ((bf16[16,3,8,8,128]{4,3,2,1,0:T(8,128)(2,1)}), bf16[16,3,8,8,128]{4,3,2,1,0:T(8,128)(2,1)S(1)}, u32[]{:S(2)}, u32[]{:S(2)}) async-start(bf16[16,3,8,8,128]{4,3,2,1,0:T(8,128)(2,1)} %choose.1), calls=%async_computation.1 | async-start | bytes 1572864 | tf_op jit(solution)/shard_map/all_to_all | solution.py:202
  30.4 14.9 %collective-permute-start = (bf16[1024,128]{1,0:T(8,128)(2,1)S(1)}, bf16[1024,128]{1,0:T(8,128)(2,1)S(1)}, u32[]{:S(2)}, u32[]{:S(2)}) collective-permute-start(bf16[1024,128]{1,0:T(8,128)(2,1)S(1)} %whiten.2.s0_ref), channel_id=1, source_target_pairs={{0,1},{1,0},{2,3},{3,2},{4,5},{5,4},{6,7},{7,6},{8,9},{9,8},{10,11... | collective-permute-start | bytes 786440 | tf_op jit(solution)/shard_map/ppermute | solution.py:192
  30.5 16.9 %collective-permute-start.5 = (bf16[1024,128]{1,0:T(8,128)(2,1)S(1)}, bf16[1024,128]{1,0:T(8,128)(2,1)S(1)}, u32[]{:S(2)}, u32[]{:S(2)}) collective-permute-start(bf16[1024,128]{1,0:T(8,128)(2,1)S(1)} %whiten.2.s0_ref), channel_id=1, source_target_pairs={{0,6},{1,7},{2,4},{3,5},{4,2},{5,3},{6,0},{7,1},{8,14},{9,15},{10,... | collective-permute-start | bytes 786440 | tf_op jit(solution)/shard_map/ppermute | solution.py:192
  31.7 17.1 %collective-permute-start.3 = (bf16[1024,128]{1,0:T(8,128)(2,1)S(1)}, bf16[1024,128]{1,0:T(8,128)(2,1)S(1)}, u32[]{:S(2)}, u32[]{:S(2)}) collective-permute-start(bf16[1024,128]{1,0:T(8,128)(2,1)S(1)} %whiten.2.s0_ref), channel_id=1, source_target_pairs={{0,4},{1,5},{2,6},{3,7},{4,0},{5,1},{6,2},{7,3},{8,12},{9,13},{10,... | collective-permute-start | bytes 786440 | tf_op jit(solution)/shard_map/ppermute | solution.py:192
  32.6 16.2 %collective-permute-start.1 = (bf16[1024,128]{1,0:T(8,128)(2,1)S(1)}, bf16[1024,128]{1,0:T(8,128)(2,1)S(1)}, u32[]{:S(2)}, u32[]{:S(2)}) collective-permute-start(bf16[1024,128]{1,0:T(8,128)(2,1)S(1)} %whiten.2.s0_ref), channel_id=1, source_target_pairs={{0,2},{1,3},{2,0},{3,1},{4,6},{5,7},{6,4},{7,5},{8,10},{9,11},{10,... | collective-permute-start | bytes 786440 | tf_op jit(solution)/shard_map/ppermute | solution.py:192
  45.3 14.0 %collective-permute-start.6 = (bf16[1024,128]{1,0:T(8,128)(2,1)S(1)}, bf16[1024,128]{1,0:T(8,128)(2,1)S(1)}, u32[]{:S(2)}, u32[]{:S(2)}) collective-permute-start(bf16[1024,128]{1,0:T(8,128)(2,1)S(1)} %collective-permute-done.s1_ref), channel_id=1, source_target_pairs={{0,6},{1,7},{2,4},{3,5},{4,2},{5,3},{6,0},{7,1},{8,14},{9,15},{10,... | collective-permute-start | bytes 786440 | tf_op jit(solution)/shard_map/ppermute | solution.py:192
  46.7 12.6 %collective-permute-start.4 = (bf16[1024,128]{1,0:T(8,128)(2,1)S(1)}, bf16[1024,128]{1,0:T(8,128)(2,1)S(1)}, u32[]{:S(2)}, u32[]{:S(2)}) collective-permute-start(bf16[1024,128]{1,0:T(8,128)(2,1)S(1)} %collective-permute-done.s1_ref), channel_id=1, source_target_pairs={{0,4},{1,5},{2,6},{3,7},{4,0},{5,1},{6,2},{7,3},{8,12},{9,13},{10,... | collective-permute-start | bytes 786440 | tf_op jit(solution)/shard_map/ppermute | solution.py:192
  47.4 12.3 %collective-permute-start.2 = (bf16[1024,128]{1,0:T(8,128)(2,1)S(1)}, bf16[1024,128]{1,0:T(8,128)(2,1)S(1)}, u32[]{:S(2)}, u32[]{:S(2)}) collective-permute-start(bf16[1024,128]{1,0:T(8,128)(2,1)S(1)} %collective-permute-done.s1_ref), channel_id=1, source_target_pairs={{0,2},{1,3},{2,0},{3,1},{4,6},{5,7},{6,4},{7,5},{8,10},{9,11},{10,... | collective-permute-start | bytes 786440 | tf_op jit(solution)/shard_map/ppermute | solution.py:192
